TPU v7x, 512 devices: a whole 4x4x16 slice. The times are simulated.
512 devices in a mesh: sector: 256 (over y, z, x_lo, core), radial: 2 (over x_hi).
Axes of the slice: x: 4 (x_hi: 2, x_lo: 2; x = x_hi * 2 + x_lo), y: 4, z: 16, core: 2. Of those that a mesh axis runs over, the one named last changes fastest.
Arguments:
- positions: float32 [8192, 512], P(('sector', 'radial')), may hold values from -6 to 6
- stiffness: float32 [8192], P(('sector', 'radial')), may hold values from 1 to 100
- blocks: bfloat16 [2, 1536, 512, 512], P(None, ('sector', 'radial')), may hold values from -0.0625 to 0.0625
- pair_src: int32 [2, 1536], P(None, ('sector', 'radial')), may hold values from 0 to 8191, as said below
- pair_tgt: int32 [2, 1536], P(None, ('sector', 'radial')), may hold values from 0 to 8191, as said below
- cross_slots: int32 [512, 1], P(('sector', 'radial')), may hold values from 0 to 15, as said below
Outputs:
- after_crossing: float32 [8192, 512], P(('sector', 'radial'))
- final_positions: float32 [8192, 512], P(('sector', 'radial'))
Inputs may be any that keep to these rules, and one draw needn't show every extreme that they name: `pair_src`: the pair at position p has its source among the 16 vesicles of the device that holds position p, that is from p // 3 * 16 on. `pair_tgt`: of the 3 pairs that a device holds, the first 1 target vesicles of the previous sector around the loop, the next 1 vesicles of its own sector, the last 1 vesicles of the next sector, in either radial sub-band. `cross_slots`: the 1 slots of a row are different.
All inputs are finite; a program needn't handle non-finite values.
Results may differ from a plain program's by a relative error of at most 0.0003.
Values may be sent and summed in bfloat16 or wider, within the bound.
A program may use at most 64 MiB of HBM per device.

v0:
```python
import functools
import math

import jax
import jax.numpy as jnp
from jax import lax
from jax.sharding import Mesh
from jax.sharding import PartitionSpec as P

ITERS = 3
SECTOR = ("sector_0", "sector_1", "sector_2", "sector_3")
SECTOR_RADIAL = ("sector_0", "sector_1", "sector_2", "sector_3", "radial")


epsilon = 1e-06


def joined_along(tiles, dim):
    shape = list(tiles.shape[1:])
    shape[dim] *= tiles.shape[0]
    return jnp.moveaxis(tiles, 0, dim).reshape(shape)


def from_everyone(array, axis):
    copies = jnp.broadcast_to(array, (lax.axis_size(axis), *array.shape))
    return lax.all_to_all(copies, axis, split_axis=0, concat_axis=0, tiled=True)


def collect(array, axis, dim):
    return joined_along(from_everyone(array, axis), dim)


def with_halo(array, sides, width):
    for axis, dim in sides:
        size, length = (lax.axis_size(axis), array.shape[dim])
        up = [(i, (i + 1) % size) for i in range(size)]
        down = [(j, i) for i, j in up]
        last = lax.slice_in_dim(array, length - width, length, axis=dim)
        initial = lax.slice_in_dim(array, 0, width, axis=dim)
        before = lax.ppermute(last, axis, up)
        after = lax.ppermute(initial, axis, down)
        array = jnp.concatenate([before, array, after], axis=dim)
    return array


def by_axis(array, axes):
    return functools.reduce(lax.psum, axes, array)


def passed_along(array, axis, by):
    length = lax.axis_size(axis)
    return lax.ppermute(array, axis, [(i, (i + by) % length) for i in range(length)])


def bending_table(points):
    wavenumber = jnp.arange(points, dtype=jnp.int32)
    frequency = jnp.minimum(wavenumber, points - wavenumber).astype(jnp.float32)
    weights = (frequency / (points // 2)) ** 4 / points
    phases = wavenumber[:, None] * wavenumber[None, :] % points
    angles = phases.astype(jnp.float32) * (2.0 * math.pi / points)
    cosines = jnp.cos(angles)
    sines = jnp.sin(angles)
    return jnp.dot(
        cosines * weights[None, :],
        cosines.T,
        preferred_element_type=jnp.float32,
        precision=lax.Precision.HIGHEST,
    ) + jnp.dot(
        sines * weights[None, :],
        sines.T,
        preferred_element_type=jnp.float32,
        precision=lax.Precision.HIGHEST,
    )


def apply_local(field, bending, fourth):
    rows = field.shape[0]
    shaped = field.reshape(rows * 2, -1)
    curved = jnp.dot(
        shaped, fourth, preferred_element_type=jnp.float32, precision=lax.Precision.HIGHEST
    ).reshape(rows, -1)
    return field + bending[:, None] * curved


def select_near(around):
    return jnp.stack([around[0], around[2], around[4]])


def local(positions, stiffness, blocks, pair_src, pair_tgt, cross_slots):
    vesicles = positions.shape[0]
    columns = positions.shape[1]
    points = columns // 2
    per_group = pair_src.shape[1] // 3
    sector = lax.axis_index(SECTOR)
    radial = lax.axis_index("radial")
    radials = lax.axis_size("radial")
    own_base = (sector * radials + radial) * vesicles
    fourth = bending_table(points)
    slot_range = jnp.arange(vesicles, dtype=jnp.int32)

    def build_near(which_step):
        id_pairs = jnp.stack([pair_src[which_step], pair_tgt[which_step]], axis=-1).reshape(
            3, 1, per_group, 2
        )
        id_band = collect(id_pairs, "radial", 1)
        id_around = with_halo(id_band, ((SECTOR, 0),), 1)
        near_ids = select_near(id_around).reshape(6 * per_group, 2)
        targets = near_ids[:, 1]
        onehot_target = (targets[:, None] - own_base == slot_range[None, :]).astype(jnp.float32)
        own_blocks = blocks[which_step]
        local_source = pair_src[which_step] - own_base
        onehot_source = (local_source[:, None] == slot_range[None, :]).astype(jnp.bfloat16)

        def near_part(field):
            rounded = field.astype(jnp.bfloat16)
            picked = jnp.dot(onehot_source, rounded, preferred_element_type=jnp.float32).astype(
                jnp.bfloat16
            )
            products = jnp.einsum(
                "pij,pj->pi", own_blocks, picked, preferred_element_type=jnp.float32
            )
            shaped_products = products.reshape(3, 1, per_group, columns)
            product_band = lax.all_gather(shaped_products, "radial", axis=1, tiled=True)
            arrived = with_halo(product_band, ((SECTOR, 0),), 1)
            received = select_near(arrived).reshape(6 * per_group, columns)
            return jnp.dot(
                onehot_target.T,
                received,
                preferred_element_type=jnp.float32,
                precision=lax.Precision.HIGHEST,
            )

        return near_part

    def solve(rhs, bending, which_step):
        near_part = build_near(which_step)
        first_norm = jnp.sqrt(by_axis(jnp.sum(rhs * rhs), SECTOR_RADIAL) + epsilon)
        krylov = [rhs / first_norm]
        hessenberg = jnp.zeros((ITERS + 1, ITERS), jnp.float32)
        for column in range(ITERS):
            field = krylov[column]
            image = apply_local(field, bending, fourth) + near_part(field)
            partials = [jnp.sum(vector * image) for vector in krylov] + [jnp.sum(image * image)]
            totals = by_axis(jnp.stack(partials), SECTOR_RADIAL)
            project = totals[: column + 1]
            for inner in range(column + 1):
                image = image - project[inner] * krylov[inner]
            remainder = jnp.maximum(totals[column + 1] - jnp.sum(project * project), 0.0)
            next_norm = jnp.sqrt(remainder + epsilon)
            hessenberg = hessenberg.at[: column + 1, column].set(project)
            hessenberg = hessenberg.at[column + 1, column].set(next_norm)
            krylov.append(image / next_norm)
        normal_matrix = jnp.dot(
            hessenberg.T,
            hessenberg,
            preferred_element_type=jnp.float32,
            precision=lax.Precision.HIGHEST,
        )
        moment = first_norm * hessenberg[0]
        factor = jnp.linalg.cholesky(normal_matrix)
        coefficients = jax.scipy.linalg.cho_solve((factor, True), moment)
        result = coefficients[0] * krylov[0]
        for column in range(1, ITERS):
            result = result + coefficients[column] * krylov[column]
        return result

    step_one = solve(positions, stiffness, 0)
    crosscount = cross_slots.shape[1]
    selector = (cross_slots[0][:, None] == slot_range[None, :]).astype(jnp.float32)
    leaving = jnp.dot(
        selector, step_one, preferred_element_type=jnp.float32, precision=lax.Precision.HIGHEST
    )
    leave_bending = jnp.dot(
        selector, stiffness, preferred_element_type=jnp.float32, precision=lax.Precision.HIGHEST
    )
    packet = jnp.concatenate(
        [leaving, jnp.pad(leave_bending, (0, columns - crosscount))[None, :]], axis=0
    )
    incoming = passed_along(packet, SECTOR, 1)
    keeping = 1.0 - jnp.sum(selector, axis=0)
    after_crossing = step_one * keeping[:, None] + jnp.dot(
        selector.T,
        incoming[:crosscount],
        preferred_element_type=jnp.float32,
        precision=lax.Precision.HIGHEST,
    )
    moved_stiffness = stiffness * keeping + jnp.dot(
        selector.T,
        incoming[crosscount, :crosscount],
        preferred_element_type=jnp.float32,
        precision=lax.Precision.HIGHEST,
    )
    final_positions = solve(after_crossing, moved_stiffness, 1)
    return (after_crossing, final_positions)


def solution(mesh):
    split = Mesh(
        mesh.devices.reshape(4, 16, 2, 2, mesh.shape["radial"]),
        ("sector_0", "sector_1", "sector_2", "sector_3", "radial"),
    )
    placed = (
        P(SECTOR_RADIAL, None),
        P(SECTOR_RADIAL),
        P(None, SECTOR_RADIAL, None, None),
        P(None, SECTOR_RADIAL),
        P(None, SECTOR_RADIAL),
        P(SECTOR_RADIAL, None),
    )
    return jax.shard_map(
        local,
        mesh=split,
        in_specs=placed,
        out_specs=(P(SECTOR_RADIAL, None), P(SECTOR_RADIAL, None)),
        check_vma=False,
    )
```

profile of v0, /device:TPU:1, one launch (start us, length us, event | category | flops | bytes accessed | tf_op | source)
XLA Modules:
  0.0 663.9 jit_solution(16376531636760542145)
XLA Ops:
  3.3 10.1 %psum.280 = f32[]{:T(128)} all-reduce(f32[]{:T(128)} %multiply_reduce_fusion.19), channel_id=1, replica_groups=mesh['sector_0'=4,'sector_1'=16,'sector_2'=2,'sector_3'=2,'radial'=2] {'..., use_global_device_ids=true, to_apply=%region_1.2 | all-reduce | flops 1 | bytes 8 | tf_op jit(solution)/shard_map/psum | solution.py:47
  13.5 29.9 %psum.281 = f32[]{:T(128)} all-reduce(f32[]{:T(128)} %psum.280), channel_id=1, replica_groups=mesh['sector_0'=4,'sector_1'=16,'sector_2'=2,'sector_3'=2,'radial'=2] {'..., use_global_device_ids=true, to_apply=%region_2.3 | all-reduce | flops 1 | bytes 8 | tf_op jit(solution)/shard_map/psum | solution.py:47
  47.7 13.8 %psum.283 = f32[]{:T(128)} all-reduce(f32[]{:T(128)} %psum.282), channel_id=1, replica_groups=mesh['sector_0'=4,'sector_1'=16,'sector_2'=2,'sector_3'=2,'radial'=2] {'..., use_global_device_ids=true, to_apply=%region_4.5 | all-reduce | flops 1 | bytes 8 | tf_op jit(solution)/shard_map/psum | solution.py:47
  109.2 7.9 %collective-permute-start.10 = (s32[1,2,1,2]{3,1,2,0:T(2,128)S(1)}, s32[1,2,1,2]{3,1,2,0:T(2,128)S(1)}, u32[]{:S(2)}, u32[]{:S(2)}) collective-permute-start(s32[1,2,1,2]{3,1,2,0:T(2,128)S(1)} %bitcast.245), channel_id=1, source_target_pairs={{2,0},{4,2},{6,4},{8,6},{10,8},{12,10},{14,12},{16,14},{18,16},{20... | collective-permute-start | bytes 56 | tf_op jit(solution)/shard_map/ppermute | solution.py:41
  131.9 20.2 %psum.286 = f32[2]{0:T(128)S(1)} all-reduce(f32[2]{0:T(128)S(1)} %psum.285), channel_id=1, replica_groups=mesh['sector_0'=4,'sector_1'=16,'sector_2'=2,'sector_3'=2,'radial'=2] {'..., use_global_device_ids=true, to_apply=%region_9.10 | all-reduce | flops 2 | bytes 16 | tf_op jit(solution)/shard_map/psum | solution.py:47
  152.6 8.2 %psum.287 = f32[2]{0:T(128)S(1)} all-reduce(f32[2]{0:T(128)S(1)} %psum.286), channel_id=1, replica_groups=mesh['sector_0'=4,'sector_1'=16,'sector_2'=2,'sector_3'=2,'radial'=2] {'..., use_global_device_ids=true, to_apply=%region_10.11 | all-reduce | flops 2 | bytes 16 | tf_op jit(solution)/shard_map/psum | solution.py:47
  160.9 13.4 %psum.288 = f32[2]{0:T(128)S(1)} all-reduce(f32[2]{0:T(128)S(1)} %psum.287), channel_id=1, replica_groups=mesh['sector_0'=4,'sector_1'=16,'sector_2'=2,'sector_3'=2,'radial'=2] {'..., use_global_device_ids=true, to_apply=%region_11.12 | all-reduce | flops 2 | bytes 16 | tf_op jit(solution)/shard_map/psum | solution.py:47
  214.6 21.5 %psum.291 = f32[3]{0:T(128)S(1)} all-reduce(f32[3]{0:T(128)S(1)} %psum.290), channel_id=1, replica_groups=mesh['sector_0'=4,'sector_1'=16,'sector_2'=2,'sector_3'=2,'radial'=2] {'..., use_global_device_ids=true, to_apply=%region_18.19 | all-reduce | flops 3 | bytes 24 | tf_op jit(solution)/shard_map/psum | solution.py:47
  236.7 9.9 %psum.292 = f32[3]{0:T(128)S(1)} all-reduce(f32[3]{0:T(128)S(1)} %psum.291), channel_id=1, replica_groups=mesh['sector_0'=4,'sector_1'=16,'sector_2'=2,'sector_3'=2,'radial'=2] {'..., use_global_device_ids=true, to_apply=%region_19.20 | all-reduce | flops 3 | bytes 24 | tf_op jit(solution)/shard_map/psum | solution.py:47
  247.2 8.1 %psum.293 = f32[3]{0:T(128)S(1)} all-reduce(f32[3]{0:T(128)S(1)} %psum.292), channel_id=1, replica_groups=mesh['sector_0'=4,'sector_1'=16,'sector_2'=2,'sector_3'=2,'radial'=2] {'..., use_global_device_ids=true, to_apply=%region_20.21 | all-reduce | flops 3 | bytes 24 | tf_op jit(solution)/shard_map/psum | solution.py:47
  296.3 21.9 %psum.296 = f32[4]{0:T(128)S(1)} all-reduce(f32[4]{0:T(128)S(1)} %psum.295), channel_id=1, replica_groups=mesh['sector_0'=4,'sector_1'=16,'sector_2'=2,'sector_3'=2,'radial'=2] {'..., use_global_device_ids=true, to_apply=%region_29.30 | all-reduce | flops 4 | bytes 32 | tf_op jit(solution)/shard_map/psum | solution.py:47
  320.8 10.1 %psum.297 = f32[4]{0:T(128)S(1)} all-reduce(f32[4]{0:T(128)S(1)} %psum.296), channel_id=1, replica_groups=mesh['sector_0'=4,'sector_1'=16,'sector_2'=2,'sector_3'=2,'radial'=2] {'..., use_global_device_ids=true, to_apply=%region_30.31 | all-reduce | flops 4 | bytes 32 | tf_op jit(solution)/shard_map/psum | solution.py:47
  332.3 8.8 %psum.298 = f32[4]{0:T(128)S(1)} all-reduce(f32[4]{0:T(128)S(1)} %psum.297), channel_id=1, replica_groups=mesh['sector_0'=4,'sector_1'=16,'sector_2'=2,'sector_3'=2,'radial'=2] {'..., use_global_device_ids=true, to_apply=%region_31.32 | all-reduce | flops 4 | bytes 32 | tf_op jit(solution)/shard_map/psum | solution.py:47
  363.6 8.3 %psum.300 = f32[]{:T(128)} all-reduce(f32[]{:T(128)} %get-tuple-element.190), channel_id=1, replica_groups=mesh['sector_0'=4,'sector_1'=16,'sector_2'=2,'sector_3'=2,'radial'=2] {'..., use_global_device_ids=true, to_apply=%region_37.0 | all-reduce | flops 1 | bytes 8 | tf_op jit(solution)/shard_map/psum | solution.py:47
  372.0 22.4 %psum.301 = f32[]{:T(128)} all-reduce(f32[]{:T(128)} %psum.300), channel_id=1, replica_groups=mesh['sector_0'=4,'sector_1'=16,'sector_2'=2,'sector_3'=2,'radial'=2] {'..., use_global_device_ids=true, to_apply=%region_38.0 | all-reduce | flops 1 | bytes 8 | tf_op jit(solution)/shard_map/psum | solution.py:47
  400.3 15.0 %psum.303 = f32[]{:T(128)} all-reduce(f32[]{:T(128)} %psum.302), channel_id=1, replica_groups=mesh['sector_0'=4,'sector_1'=16,'sector_2'=2,'sector_3'=2,'radial'=2] {'..., use_global_device_ids=true, to_apply=%region_40.43 | all-reduce | flops 1 | bytes 8 | tf_op jit(solution)/shard_map/psum | solution.py:47
  448.3 21.5 %psum.306 = f32[2]{0:T(128)S(1)} all-reduce(f32[2]{0:T(128)S(1)} %psum.305), channel_id=1, replica_groups=mesh['sector_0'=4,'sector_1'=16,'sector_2'=2,'sector_3'=2,'radial'=2] {'..., use_global_device_ids=true, to_apply=%region_45.48 | all-reduce | flops 2 | bytes 16 | tf_op jit(solution)/shard_map/psum | solution.py:47
  469.8 10.9 %psum.307 = f32[2]{0:T(128)S(1)} all-reduce(f32[2]{0:T(128)S(1)} %psum.306), channel_id=1, replica_groups=mesh['sector_0'=4,'sector_1'=16,'sector_2'=2,'sector_3'=2,'radial'=2] {'..., use_global_device_ids=true, to_apply=%region_46.49 | all-reduce | flops 2 | bytes 16 | tf_op jit(solution)/shard_map/psum | solution.py:47
  480.7 8.0 %psum.308 = f32[2]{0:T(128)S(1)} all-reduce(f32[2]{0:T(128)S(1)} %psum.307), channel_id=1, replica_groups=mesh['sector_0'=4,'sector_1'=16,'sector_2'=2,'sector_3'=2,'radial'=2] {'..., use_global_device_ids=true, to_apply=%region_47.50 | all-reduce | flops 2 | bytes 16 | tf_op jit(solution)/shard_map/psum | solution.py:47
  526.9 21.5 %psum.311 = f32[3]{0:T(128)S(1)} all-reduce(f32[3]{0:T(128)S(1)} %psum.310), channel_id=1, replica_groups=mesh['sector_0'=4,'sector_1'=16,'sector_2'=2,'sector_3'=2,'radial'=2] {'..., use_global_device_ids=true, to_apply=%region_53.56 | all-reduce | flops 3 | bytes 24 | tf_op jit(solution)/shard_map/psum | solution.py:47
  548.3 10.1 %psum.312 = f32[3]{0:T(128)S(1)} all-reduce(f32[3]{0:T(128)S(1)} %psum.311), channel_id=1, replica_groups=mesh['sector_0'=4,'sector_1'=16,'sector_2'=2,'sector_3'=2,'radial'=2] {'..., use_global_device_ids=true, to_apply=%region_54.57 | all-reduce | flops 3 | bytes 24 | tf_op jit(solution)/shard_map/psum | solution.py:47
  558.4 7.9 %psum.313 = f32[3]{0:T(128)S(1)} all-reduce(f32[3]{0:T(128)S(1)} %psum.312), channel_id=1, replica_groups=mesh['sector_0'=4,'sector_1'=16,'sector_2'=2,'sector_3'=2,'radial'=2] {'..., use_global_device_ids=true, to_apply=%region_55.58 | all-reduce | flops 3 | bytes 24 | tf_op jit(solution)/shard_map/psum | solution.py:47
  604.0 22.1 %psum.316 = f32[4]{0:T(128)S(1)} all-reduce(f32[4]{0:T(128)S(1)} %psum.315), channel_id=1, replica_groups=mesh['sector_0'=4,'sector_1'=16,'sector_2'=2,'sector_3'=2,'radial'=2] {'..., use_global_device_ids=true, to_apply=%region_63.66 | all-reduce | flops 4 | bytes 32 | tf_op jit(solution)/shard_map/psum | solution.py:47
  628.1 10.0 %psum.317 = f32[4]{0:T(128)S(1)} all-reduce(f32[4]{0:T(128)S(1)} %psum.316), channel_id=1, replica_groups=mesh['sector_0'=4,'sector_1'=16,'sector_2'=2,'sector_3'=2,'radial'=2] {'..., use_global_device_ids=true, to_apply=%region_64.67 | all-reduce | flops 4 | bytes 32 | tf_op jit(solution)/shard_map/psum | solution.py:47
  (255 shorter events, 310.3 us)
Async XLA Ops:
  63.5 30.3 %all-to-all-start = ((s32[2,3,1,1,2]{1,4,3,2,0:T(2,128)}), s32[2,3,1,1,2]{1,4,3,2,0:T(2,128)S(1)}, u32[]{:S(2)}, u32[]{:S(2)}) async-start(s32[2,3,1,1,2]{1,4,3,2,0:T(2,128)} %broadcast_in_dim.6), calls=%async_computation | async-start | bytes 4096 | tf_op jit(solution)/shard_map/all_to_all | solution.py:26
  75.2 107.7 %copy-start.1 = (f32[16,512]{1,0:T(8,128)S(1)}, f32[16,512]{1,0:T(8,128)}, u32[]{:S(2)}) copy-start(f32[16,512]{1,0:T(8,128)} %param.33) | copy-start | bytes 98308
  77.1 107.1 %copy-start = (bf16[2,3,512,512]{3,2,1,0:T(8,128)(2,1)S(1)}, bf16[2,3,512,512]{3,2,1,0:T(8,128)(2,1)}, u32[]{:S(2)}) copy-start(bf16[2,3,512,512]{3,2,1,0:T(8,128)(2,1)} %param.35) | copy-start | bytes 9437188
  82.0 38.9 %collective-permute-start.2 = (f32[1,2,1,512]{3,1,2,0:T(2,128)S(1)}, f32[1,2,1,512]{3,1,2,0:T(2,128)}, u32[]{:S(2)}, u32[]{:S(2)}) collective-permute-start(f32[1,2,1,512]{3,1,2,0:T(2,128)S(1)} %reshape.597), channel_id=1, source_target_pairs={{0,2},{2,4},{4,6},{6,8},{8,10},{10,12},{12,14},{14,16},{16,18},{18... | collective-permute-start | bytes 12296 | tf_op jit(solution)/shard_map/ppermute | solution.py:40
  87.5 33.4 %collective-permute-start.3 = (f32[1,2,1,512]{3,1,2,0:T(2,128)}, f32[1,2,1,512]{3,1,2,0:T(2,128)}, u32[]{:S(2)}, u32[]{:S(2)}) collective-permute-start(f32[1,2,1,512]{3,1,2,0:T(2,128)} %reshape.599), channel_id=1, source_target_pairs={{2,0},{4,2},{6,4},{8,6},{10,8},{12,10},{14,12},{16,14},{18,16},{20... | collective-permute-start | bytes 12296 | tf_op jit(solution)/shard_map/ppermute | solution.py:41
  94.4 14.6 %all-to-all-start.1 = ((s32[2,3,1,1,2]{1,4,3,2,0:T(2,128)}), s32[2,3,1,1,2]{1,4,3,2,0:T(2,128)S(1)}, u32[]{:S(2)}, u32[]{:S(2)}) async-start(s32[2,3,1,1,2]{1,4,3,2,0:T(2,128)} %broadcast_in_dim.8), calls=%async_computation.1 | async-start | bytes 4096 | tf_op jit(solution)/shard_map/all_to_all | solution.py:26
  99.7 17.4 %collective-permute-start = (s32[1,2,1,2]{3,1,2,0:T(2,128)S(1)}, s32[1,2,1,2]{3,1,2,0:T(2,128)S(1)}, u32[]{:S(2)}, u32[]{:S(2)}) collective-permute-start(s32[1,2,1,2]{3,1,2,0:T(2,128)S(1)} %bitcast.246), channel_id=1, source_target_pairs={{0,2},{2,4},{4,6},{6,8},{8,10},{10,12},{12,14},{14,16},{16,18},{18... | collective-permute-start | bytes 56 | tf_op jit(solution)/shard_map/ppermute | solution.py:40
  103.0 16.0 %collective-permute-start.1 = (s32[1,2,1,2]{3,1,2,0:T(2,128)S(1)}, s32[1,2,1,2]{3,1,2,0:T(2,128)S(1)}, u32[]{:S(2)}, u32[]{:S(2)}) collective-permute-start(s32[1,2,1,2]{3,1,2,0:T(2,128)S(1)} %bitcast.243), channel_id=1, source_target_pairs={{2,0},{4,2},{6,4},{8,6},{10,8},{12,10},{14,12},{16,14},{18,16},{20... | collective-permute-start | bytes 56 | tf_op jit(solution)/shard_map/ppermute | solution.py:41
  109.2 9.8 %collective-permute-start.10 = (s32[1,2,1,2]{3,1,2,0:T(2,128)S(1)}, s32[1,2,1,2]{3,1,2,0:T(2,128)S(1)}, u32[]{:S(2)}, u32[]{:S(2)}) collective-permute-start(s32[1,2,1,2]{3,1,2,0:T(2,128)S(1)} %bitcast.245), channel_id=1, source_target_pairs={{2,0},{4,2},{6,4},{8,6},{10,8},{12,10},{14,12},{16,14},{18,16},{20... | collective-permute-start | bytes 56 | tf_op jit(solution)/shard_map/ppermute | solution.py:41
  117.1 3.1 collective-permute-start.9
  120.9 61.9 %copy-start.6 = (s32[6,1]{0,1:T(1,128)}, s32[6,1]{0,1:T(1,128)S(1)}, u32[]{:S(2)}) copy-start(s32[6,1]{0,1:T(1,128)S(1)} %copy.54) | copy-start | bytes 76
  189.5 7.9 %collective-permute-start.4 = (f32[1,2,1,512]{3,1,2,0:T(2,128)S(1)}, f32[1,2,1,512]{3,1,2,0:T(2,128)}, u32[]{:S(2)}, u32[]{:S(2)}) collective-permute-start(f32[1,2,1,512]{3,1,2,0:T(2,128)S(1)} %reshape.600), channel_id=1, source_target_pairs={{0,2},{2,4},{4,6},{6,8},{8,10},{10,12},{12,14},{14,16},{16,18},{18... | collective-permute-start | bytes 12296 | tf_op jit(solution)/shard_map/ppermute | solution.py:40
  193.4 5.3 collective-permute-start.5
  273.2 9.2 %collective-permute-start.6 = (f32[1,2,1,512]{3,1,2,0:T(2,128)S(1)}, f32[1,2,1,512]{3,1,2,0:T(2,128)}, u32[]{:S(2)}, u32[]{:S(2)}) collective-permute-start(f32[1,2,1,512]{3,1,2,0:T(2,128)S(1)} %reshape.603), channel_id=1, source_target_pairs={{0,2},{2,4},{4,6},{6,8},{8,10},{10,12},{12,14},{14,16},{16,18},{18... | collective-permute-start | bytes 12296 | tf_op jit(solution)/shard_map/ppermute | solution.py:40
  277.1 5.3 collective-permute-start.7
  358.5 3.8 collective-permute-start.8
  363.6 297.8 %copy-start.2 = (f32[16,512]{1,0:T(8,128)}, f32[16,512]{1,0:T(8,128)S(1)}, u32[]{:S(2)}) copy-start(f32[16,512]{1,0:T(8,128)S(1)} %get-tuple-element.191) | copy-start | bytes 98308
  416.0 82.9 %copy-start.5 = (s32[6,1]{0,1:T(1,128)}, s32[6,1]{0,1:T(1,128)S(1)}, u32[]{:S(2)}) copy-start(s32[6,1]{0,1:T(1,128)S(1)} %copy.55) | copy-start | bytes 76
  429.3 8.7 %collective-permute-start.11 = (f32[1,2,1,512]{3,1,2,0:T(2,128)S(1)}, f32[1,2,1,512]{3,1,2,0:T(2,128)S(1)}, u32[]{:S(2)}, u32[]{:S(2)}) collective-permute-start(f32[1,2,1,512]{3,1,2,0:T(2,128)S(1)} %reshape.606), channel_id=1, source_target_pairs={{0,2},{2,4},{4,6},{6,8},{8,10},{10,12},{12,14},{14,16},{16,18},{18... | collective-permute-start | bytes 12296 | tf_op jit(solution)/shard_map/ppermute | solution.py:40
  433.1 5.2 collective-permute-start.12
  503.7 7.9 %collective-permute-start.13 = (f32[1,2,1,512]{3,1,2,0:T(2,128)S(1)}, f32[1,2,1,512]{3,1,2,0:T(2,128)}, u32[]{:S(2)}, u32[]{:S(2)}) collective-permute-start(f32[1,2,1,512]{3,1,2,0:T(2,128)S(1)} %reshape.609), channel_id=1, source_target_pairs={{0,2},{2,4},{4,6},{6,8},{8,10},{10,12},{12,14},{14,16},{16,18},{18... | collective-permute-start | bytes 12296 | tf_op jit(solution)/shard_map/ppermute | solution.py:40
  507.6 5.3 collective-permute-start.14
  583.1 7.3 %collective-permute-start.15 = (f32[1,2,1,512]{3,1,2,0:T(2,128)S(1)}, f32[1,2,1,512]{3,1,2,0:T(2,128)S(1)}, u32[]{:S(2)}, u32[]{:S(2)}) collective-permute-start(f32[1,2,1,512]{3,1,2,0:T(2,128)S(1)} %reshape.612), channel_id=1, source_target_pairs={{0,2},{2,4},{4,6},{6,8},{8,10},{10,12},{12,14},{14,16},{16,18},{18... | collective-permute-start | bytes 12296 | tf_op jit(solution)/shard_map/ppermute | solution.py:40
  587.0 5.2 collective-permute-start.16
  (4 other events, 135.2 us)
where the time goes:
time: 668 us; the launch traced here: 664 us
  blocking collectives  467 us (70%)
  starting transfers between devices  68.7 us (10%)
  other arithmetic  52.5 us (8%)
  matrix products  28.1 us (4%)
  local copies, waits for them, and re-layouts  27.9 us (4%)
  between operations  12.3 us (2%)
  waiting for transfers between devices  7.1 us (1%)
    psum x40, blocking collectives, by_axis(): return functools.reduce(lax.psum, axes, array)  439 us
    ppermute x8, starting transfers between devices, with_halo(): before = lax.ppermute(last, axis, up)  29.5 us
    all_gather x6, blocking collectives, near_part(): product_band = lax.all_gather(shaped_products, 'radial', axis=1, tiled=True)  28.4 us
    ppermute x8, starting transfers between devices, with_halo(): after = lax.ppermute(initial, axis, down)  27.4 us
  transfers between devices with their start and end apart: 19, of which 6 were waited for; matrix products, arithmetic and copies ran while one was open for 3% of the time, Pallas kernels for 0%

commit v1 on v0

v1 whole, which is shorter than its diff:
```python
import functools

import jax
import jax.numpy as jnp
import numpy as np
from jax import lax
from jax.experimental import pallas as pl
from jax.experimental.pallas import tpu as pltpu
from jax.sharding import Mesh
from jax.sharding import PartitionSpec as P

ITERS = 3
SECTOR = ("sector_0", "sector_1", "sector_2", "sector_3")
SECTOR_RADIAL = ("sector_0", "sector_1", "sector_2", "sector_3", "radial")
MESH = pl.DeviceIdType.MESH
EPSILON = 1e-06
GAMMA = 64.0
PAIRS_IN = 3
LINKS = 5


def bending_table(points):
    k = np.arange(points)
    weights = (np.minimum(k, points - k) / (points // 2)) ** 4 / points
    angles = (k[:, None] * k[None, :] % points) * (2.0 * np.pi / points)
    table = (np.cos(angles) * weights) @ np.cos(angles).T + (np.sin(angles) * weights) @ np.sin(angles).T
    return table.astype(np.float32)


def dot_nt(a, b, precision=None):
    return lax.dot_general(
        a, b, (((1,), (1,)), ((), ())), preferred_element_type=jnp.float32, precision=precision
    )


def total_of(terms):
    terms = list(terms)
    return functools.reduce(lambda a, b: a + b, terms)


def krylov_weights(gram):
    at = lambda i, j: gram[(min(i, j), max(i, j))]
    first = jnp.sqrt(at(0, 0) + EPSILON)
    basis = [[1.0 / first]]
    hess = {}
    for j in range(ITERS):
        image = [GAMMA * a for a in basis[j]]
        seen = [total_of(at(i, m + 1) * image[m] for m in range(j + 1)) for i in range(j + 1)]
        h = [total_of(basis[i][a] * seen[a] for a in range(i + 1)) for i in range(j + 1)]
        left = []
        for a in range(j + 2):
            value = image[a - 1] if a > 0 else None
            for i in range(a, j + 1):
                term = h[i] * basis[i][a]
                value = -term if value is None else value - term
            left.append(value)
        square = total_of(
            left[a] * total_of(at(a, b) * left[b] for b in range(j + 2)) for a in range(j + 2)
        )
        norm = jnp.sqrt(jnp.maximum(square, 0.0) + EPSILON)
        for i in range(j + 1):
            hess[(i, j)] = h[i]
        hess[(j + 1, j)] = norm
        scale = 1.0 / norm
        basis.append([a * scale for a in left])
    normal = {}
    for i in range(ITERS):
        for j in range(i + 1):
            normal[(i, j)] = total_of(hess[(k, i)] * hess[(k, j)] for k in range(min(i, j) + 2))
    moment = [first * hess[(0, j)] for j in range(ITERS)]
    factor, inverse = {}, []
    for i in range(ITERS):
        for j in range(i):
            value = normal[(i, j)]
            for k in range(j):
                value = value - factor[(i, k)] * factor[(j, k)]
            factor[(i, j)] = value * inverse[j]
        value = normal[(i, i)]
        for k in range(i):
            value = value - factor[(i, k)] * factor[(i, k)]
        inverse.append(1.0 / jnp.sqrt(value))
    forward = []
    for i in range(ITERS):
        value = moment[i]
        for k in range(i):
            value = value - factor[(i, k)] * forward[k]
        forward.append(value * inverse[i])
    coefficients = [None] * ITERS
    for i in reversed(range(ITERS)):
        value = forward[i]
        for k in range(i + 1, ITERS):
            value = value - factor[(k, i)] * coefficients[k]
        coefficients[i] = value * inverse[i]
    return [
        total_of(coefficients[j] * basis[j][a] for j in range(a, ITERS)) for a in range(ITERS)
    ]


def kernel(
    sizes,
    src_ref,
    tgt_ref,
    slot_ref,
    pos_ref,
    stiff_ref,
    fourth_ref,
    blocks_ref,
    after_ref,
    final_ref,
    block_buf,
    id_out,
    id_in,
    near_out,
    near_in,
    row_out,
    row_in,
    gram_buf,
    scalar_buf,
    sum_out,
    sum_in_0,
    sum_in_1,
    sum_in_2,
    block_sem,
    id_send,
    id_recv,
    near_send,
    near_recv,
    row_send,
    row_recv,
    sum_send,
    sum_recv,
):
    ny, nz, nx, nc, nr = sizes
    rows, columns = pos_ref.shape
    points = columns // 2
    y, z, x, c, r = (lax.axis_index(name) for name in SECTOR_RADIAL)
    sectors = ny * nz * nx * nc
    sector = ((y * nz + z) * nx + x) * nc + c
    own_base = (sector * nr + r) * rows

    def place(index, radial):
        return (
            lax.div(index, nc * nx * nz),
            lax.rem(lax.div(index, nc * nx), nz),
            lax.rem(lax.div(index, nc), nx),
            lax.rem(index, nc),
            radial,
        )

    before = lax.rem(sector + sectors - 1, sectors)
    after = lax.rem(sector + 1, sectors)
    other = lax.rem(r + 1, nr)
    links = [
        (0, place(before, r)),
        (0, place(before, other)),
        (1, (y, z, x, c, other)),
        (2, place(after, r)),
        (2, place(after, other)),
    ]

    stage_0 = [
        (lax.rem(x + i, nx), lax.rem(c + j, nc), lax.rem(r + k, nr))
        for i in range(nx)
        for j in range(nc)
        for k in range(nr)
    ][1:]
    stages = [
        [(y, z, a, b, d) for a, b, d in stage_0],
        [(lax.rem(y + i, ny), z, x, c, r) for i in range(1, ny)],
        [(y, lax.rem(z + i, nz), x, c, r) for i in range(1, nz)],
    ]

    loads = [
        pltpu.make_async_copy(blocks_ref.at[k], block_buf.at[k], block_sem.at[k]) for k in range(2)
    ]
    for load in loads:
        load.start()

    barrier = pltpu.get_barrier_semaphore()
    greeted = [device for _, device in links] + [device for stage in stages for device in stage]
    for device in greeted:
        pl.semaphore_signal(barrier, inc=1, device_id=device, device_id_type=MESH)

    lane = lax.broadcasted_iota(jnp.int32, (1, 128), 1)
    row_of = lax.broadcasted_iota(jnp.int32, (rows, 1), 0)
    row_wide = lax.broadcasted_iota(jnp.int32, (rows, columns), 0)
    eye = lax.broadcasted_iota(jnp.int32, (rows, rows), 0) == lax.broadcasted_iota(
        jnp.int32, (rows, rows), 1
    )
    stiff_row = stiff_ref[...]
    stiff = jnp.sum(jnp.where(eye, stiff_row, 0.0), axis=1, keepdims=True)
    slot = slot_ref[0, 0]
    leaving_stiff = jnp.sum(jnp.where(row_of == slot, stiff, 0.0), axis=0, keepdims=True)

    ids = jnp.where(lane == 6, leaving_stiff, 0.0)
    for k in range(2):
        for p in range(PAIRS_IN):
            ids = jnp.where(lane == k * PAIRS_IN + p, tgt_ref[k, p].astype(jnp.float32), ids)
    id_out[...] = ids

    pl.semaphore_wait(barrier, len(greeted))

    def send(source, target, send_sem, recv_sem, device):
        copy = pltpu.make_async_remote_copy(
            src_ref=source,
            dst_ref=target,
            send_sem=send_sem,
            recv_sem=recv_sem,
            device_id=device,
            device_id_type=MESH,
        )
        copy.start()
        return copy

    sent = []
    id_copies = [
        send(id_out, id_in.at[l], id_send.at[l], id_recv.at[l], device)
        for l, (_, device) in enumerate(links)
    ]
    sent += id_copies

    def targets_of(k):
        masks = []
        for l, (pair, _) in enumerate(links):
            target = jnp.sum(
                jnp.where(lane == k * PAIRS_IN + pair, id_in[l], 0.0), axis=1, keepdims=True
            )
            masks.append(row_of == target.astype(jnp.int32) - own_base)
        masks.append(row_of == tgt_ref[k, 1] - own_base)
        return [mask.astype(jnp.float32) for mask in masks]

    fourth = fourth_ref[...]
    operand_row = lax.broadcasted_iota(jnp.int32, (8, columns), 0)

    def apply(field, bending, k, exchange, masks):
        products = []
        for p in range(PAIRS_IN):
            source = src_ref[k, p] - own_base
            picked = jnp.sum(jnp.where(row_wide == source, field, 0.0), axis=0, keepdims=True)
            high = picked.astype(jnp.bfloat16).astype(jnp.float32)
            low = picked - high
            operand = jnp.where(
                operand_row == 0, high, jnp.where(operand_row == 1, low, 0.0)
            ).astype(jnp.bfloat16)
            product = jnp.sum(dot_nt(operand, block_buf[k, p]), axis=0, keepdims=True)
            near_out[exchange, p] = product
            products.append(product)
        copies = [
            send(
                near_out.at[exchange, pair],
                near_in.at[exchange, l],
                near_send.at[exchange, l],
                near_recv.at[exchange, l],
                device,
            )
            for l, (pair, device) in enumerate(links)
        ]
        sent.extend(copies)
        shaped = jnp.concatenate([field[:, :points], field[:, points:]], axis=0)
        curved = jnp.dot(
            shaped, fourth, preferred_element_type=jnp.float32, precision=lax.Precision.HIGHEST
        )
        curved = jnp.concatenate([curved[:rows], curved[rows:]], axis=1)
        image = field + bending * curved
        if masks is None:
            for copy in id_copies:
                copy.wait_recv()
            masks = targets_of(k)
        image = image + masks[LINKS] * products[1]
        for l, copy in enumerate(copies):
            copy.wait_recv()
            image = image + masks[l] * near_in[exchange, l]
        return image * (1.0 / GAMMA), masks

    def everywhere(values, which):
        for t, (stage, inbox) in enumerate(zip(stages, (sum_in_0, sum_in_1, sum_in_2))):
            if not stage:
                continue
            sum_out[which, t] = values
            first = sum(len(s) for s in stages[:t])
            copies = [
                send(
                    sum_out.at[which, t],
                    inbox.at[which, i],
                    sum_send.at[which, first + i],
                    sum_recv.at[which, first + i],
                    device,
                )
                for i, device in enumerate(stage)
            ]
            sent.extend(copies)
            for i, copy in enumerate(copies):
                copy.wait_recv()
                values = values + inbox[which, i]
        diagonal = lax.broadcasted_iota(jnp.int32, (128, 128), 0) == lax.broadcasted_iota(
            jnp.int32, (128, 128), 1
        )
        spread = jnp.dot(
            jnp.where(diagonal, values, 0.0),
            jnp.ones((128, 128), jnp.float32),
            preferred_element_type=jnp.float32,
            precision=lax.Precision.HIGHEST,
        )
        scalar_buf[...] = spread

    def folded(product):
        wide = sum(product[:, i * 128 : (i + 1) * 128] for i in range(columns // 128))
        return jnp.sum(wide, axis=0, keepdims=True)

    gram_buf[...] = jnp.zeros_like(gram_buf)

    def solve(start, bending, k, masks):
        basis = [start]
        for j in range(ITERS):
            image, masks = apply(basis[j], bending, k, k * ITERS + j, masks)
            basis.append(image)
        pairs = [(i, j) for i in range(ITERS + 1) for j in range(i, ITERS + 1)]
        for n, (i, j) in enumerate(pairs):
            gram_buf[n : n + 1, :] = folded(basis[i] * basis[j])
        sums = dot_nt(jnp.ones((8, 128), jnp.float32), gram_buf[...], lax.Precision.HIGHEST)
        everywhere(sums[0:1], k)
        weights = krylov_weights(
            {pair: scalar_buf[n : n + 1, :] for n, pair in enumerate(pairs)}
        )
        return total_of(
            jnp.broadcast_to(weights[a][:, 0:1], (rows, columns)) * basis[a] for a in range(ITERS)
        )

    for load in loads:
        load.wait()
    step_one = solve(pos_ref[...], stiff, 0, None)
    row_out[0] = jnp.sum(jnp.where(row_wide == slot, step_one, 0.0), axis=0, keepdims=True)
    crossing = send(row_out.at[0], row_in.at[0], row_send.at[0], row_recv.at[0], links[3][1])
    sent.append(crossing)
    masks = targets_of(1)
    new_stiff = jnp.sum(jnp.where(lane == 6, id_in[3], 0.0), axis=1, keepdims=True)
    moved_stiff = jnp.where(row_of == slot, new_stiff, stiff)
    crossing.wait_recv()
    crossed = jnp.where(row_wide == slot, row_in[0], step_one)
    after_ref[...] = crossed
    final_ref[...] = solve(crossed, moved_stiff, 1, masks)
    for copy in sent:
        copy.wait_send()


def local(sizes, table, positions, stiffness, blocks, pair_src, pair_tgt, cross_slots):
    rows, columns = positions.shape
    ny, nz, nx, nc, nr = sizes
    peers = (nx * nc * nr - 1, ny - 1, nz - 1)
    vmem = pl.BlockSpec(memory_space=pltpu.VMEM)
    smem = pl.BlockSpec(memory_space=pltpu.SMEM)
    f32 = jnp.float32
    dma = pltpu.SemaphoreType.DMA
    return pl.pallas_call(
        functools.partial(kernel, sizes),
        out_shape=(jax.ShapeDtypeStruct((rows, columns), f32),) * 2,
        in_specs=[smem, smem, smem, vmem, vmem, vmem, pl.BlockSpec(memory_space=pl.ANY)],
        out_specs=(vmem, vmem),
        scratch_shapes=[
            pltpu.VMEM(blocks.shape, blocks.dtype),
            pltpu.VMEM((1, 128), f32),
            pltpu.VMEM((LINKS, 1, 128), f32),
            pltpu.VMEM((2 * ITERS, PAIRS_IN, 1, columns), f32),
            pltpu.VMEM((2 * ITERS, LINKS, 1, columns), f32),
            pltpu.VMEM((1, 1, columns), f32),
            pltpu.VMEM((1, 1, columns), f32),
            pltpu.VMEM((128, 128), f32),
            pltpu.VMEM((128, 128), f32),
            pltpu.VMEM((2, 3, 1, 128), f32),
            pltpu.VMEM((2, max(peers[0], 1), 1, 128), f32),
            pltpu.VMEM((2, max(peers[1], 1), 1, 128), f32),
            pltpu.VMEM((2, max(peers[2], 1), 1, 128), f32),
            dma((2,)),
            dma((LINKS,)),
            dma((LINKS,)),
            dma((2 * ITERS, LINKS)),
            dma((2 * ITERS, LINKS)),
            dma((1,)),
            dma((1,)),
            dma((2, sum(peers))),
            dma((2, sum(peers))),
        ],
        compiler_params=pltpu.CompilerParams(collective_id=0, has_side_effects=True),
    )(
        pair_src,
        pair_tgt,
        cross_slots,
        positions,
        stiffness.reshape(1, rows),
        jnp.asarray(table),
        blocks,
    )


def program(split):
    sizes = tuple(split.shape[name] for name in SECTOR_RADIAL)
    placed = (
        P(SECTOR_RADIAL, None),
        P(SECTOR_RADIAL),
        P(None, SECTOR_RADIAL, None, None),
        P(None, SECTOR_RADIAL),
        P(None, SECTOR_RADIAL),
        P(SECTOR_RADIAL, None),
    )
    return jax.shard_map(
        functools.partial(local, sizes, bending_table(256)),
        mesh=split,
        in_specs=placed,
        out_specs=(P(SECTOR_RADIAL, None), P(SECTOR_RADIAL, None)),
        check_vma=False,
    )


def solution(mesh):
    split = Mesh(mesh.devices.reshape(4, 16, 2, 2, mesh.shape["radial"]), SECTOR_RADIAL)
    return program(split)
```

time: 668 us -> 80.5 us (0.12)
  blocking collectives: 467 us -> 0 us
  Pallas kernels: 0 us -> 76.2 us
  starting transfers between devices: 68.7 us -> 0 us
  other arithmetic: 52.5 us -> 0 us
  matrix products: 28.1 us -> 0 us
  local copies, waits for them, and re-layouts: 27.9 us -> 2.75 us
  between operations: 12.3 us -> 1.29 us
  waiting for transfers between devices: 7.1 us -> 0 us
    psum x40 -> x0, blocking collectives: 439 us -> none  [by_axis(): return functools.reduce(lax.psum, axes, array)]
    pallas_call x0 -> x1, Pallas kernels: none -> 76.2 us  [local(): pl.pallas_call(functools.partial(kernel, sizes), out_shape=(jax.ShapeDtyp...]
    ppermute x17 -> x0, starting transfers between devices: 59.5 us -> none  [the longest x8 29.5 us: with_halo(): before = lax.ppermute(last, axis, up)]
    another operation x35 -> x0, other arithmetic: 32.4 us -> none  [the longest x6 11.6 us: solve(): totals = by_axis(jnp.stack(partials), SECTOR_RADIAL)]
    all_gather x6 -> x0, blocking collectives: 28.4 us -> none  [near_part(): product_band = lax.all_gather(shaped_products, 'radial', axis=1, tiled=True)]
    dot_general x29 -> x0, matrix products: 27.6 us -> none  [the longest x6 11.1 us: near_part(): jnp.dot(onehot_target.T, received, preferred_element_type=jnp.float32, pr...]
    all_to_all x2 -> x0, starting transfers between devices: 9.14 us -> none  [from_everyone(): return lax.all_to_all(copies, axis, split_axis=0, concat_axis=0, tiled=True)]
    reshape x20 -> x0, local copies, waits for them, and re-layouts: 7.67 us -> none  [the longest x6 4.18 us: apply_local(): curved = jnp.dot(shaped, fourth, preferred_element_type=jnp.float32, prec...]
  transfers between devices with their start and end apart: 19 -> 0, of which waited for: 6 -> 0; matrix products, arithmetic and copies ran while one was open for 3% -> 0% of each run, Pallas kernels for 0% -> 0%
where the time goes in v1:
time: 80.5 us; the launch traced here: 80.2 us
  Pallas kernels  76.2 us (95%)
  local copies, waits for them, and re-layouts  2.75 us (3%)
  between operations  1.29 us (2%)
    pallas_call x1, Pallas kernels, local(): pl.pallas_call(functools.partial(kernel, sizes), out_shape=(jax.ShapeDtyp...  76.2 us
    unnamed x2, local copies, waits for them, and re-layouts  2.75 us

profile of v1, /device:TPU:1, one launch (start us, length us, event | category | flops | bytes accessed | tf_op | source)
XLA Modules:
  0.0 80.2 jit_solution(9099422888203152397)
XLA Ops:
  1.3 76.2 %shard_map.86 = (f32[16,512]{1,0:T(8,128)}, f32[16,512]{1,0:T(8,128)}) custom-call(s32[2,3]{1,0:T(2,128)} %src_ref.1, s32[2,3]{1,0:T(2,128)} %tgt_ref.1, s32[1,1]{1,0:T(1,128)S(6)} %copy.11.slot_ref, f32[16,512]{1,0:T(8,128)} %pos_ref.1, f32[1,16]{1,0:T(1,128)} %bitcast.1, f32[256,256]{1,0:T(8,128)} %constant.2.clone.fourth_ref, ...), custom_call_target="tpu_custom_call" | custom-call | tf_op jit(solution)/shard_map/pallas_call | solution.py:354
  77.4 1.4 %copy.12 = f32[16,512]{1,0:T(8,128)} copy(f32[16,512]{1,0:T(8,128)} %get-tuple-element.4) | data formatting | bytes 65536
  78.8 1.4 %copy.13 = f32[16,512]{1,0:T(8,128)} copy(f32[16,512]{1,0:T(8,128)} %get-tuple-element.5) | data formatting | bytes 65536

commit v2 on v1

--- a/solution.py
+++ b/solution.py
@@ -112,6 +112,8 @@
     id_in,
     near_out,
     near_in,
+    wide_out,
+    wide_in,
     row_out,
     row_in,
     gram_buf,
@@ -198,8 +200,6 @@
             ids = jnp.where(lane == k * PAIRS_IN + p, tgt_ref[k, p].astype(jnp.float32), ids)
     id_out[...] = ids
 
-    pl.semaphore_wait(barrier, len(greeted))
-
     def send(source, target, send_sem, recv_sem, device):
         copy = pltpu.make_async_remote_copy(
             src_ref=source,
@@ -213,12 +213,6 @@
         return copy
 
     sent = []
-    id_copies = [
-        send(id_out, id_in.at[l], id_send.at[l], id_recv.at[l], device)
-        for l, (_, device) in enumerate(links)
-    ]
-    sent += id_copies
-
     def targets_of(k):
         masks = []
         for l, (pair, _) in enumerate(links):
@@ -232,23 +226,34 @@
     fourth = fourth_ref[...]
     operand_row = lax.broadcasted_iota(jnp.int32, (8, columns), 0)
 
-    def apply(field, bending, k, exchange, masks):
-        products = []
+    def pick(fields, k, exchange):
+        out = near_out.at[exchange] if len(fields) == 1 else wide_out.at[exchange - ITERS]
+        own = None
         for p in range(PAIRS_IN):
-            source = src_ref[k, p] - own_base
-            picked = jnp.sum(jnp.where(row_wide == source, field, 0.0), axis=0, keepdims=True)
-            high = picked.astype(jnp.bfloat16).astype(jnp.float32)
-            low = picked - high
-            operand = jnp.where(
-                operand_row == 0, high, jnp.where(operand_row == 1, low, 0.0)
-            ).astype(jnp.bfloat16)
-            product = jnp.sum(dot_nt(operand, block_buf[k, p]), axis=0, keepdims=True)
-            near_out[exchange, p] = product
-            products.append(product)
+            mask = row_wide == src_ref[k, p] - own_base
+            stacked = jnp.zeros((8, columns), jnp.float32)
+            for j, field in enumerate(fields):
+                picked = jnp.sum(jnp.where(mask, field, 0.0), axis=0, keepdims=True)
+                stacked = jnp.where(lax.rem(operand_row, 4) == j, picked, stacked)
+            high = stacked.astype(jnp.bfloat16).astype(jnp.float32)
+            operand = jnp.where(operand_row < 4, high, stacked - high).astype(jnp.bfloat16)
+            product = dot_nt(operand, block_buf[k, p])
+            product = product[0:4] + product[4:8]
+            if len(fields) == 1:
+                product = product[0:1]
+            out[p] = product
+            if p == 1:
+                own = product
+        return own
+
+    def launch(exchange):
+        wide = exchange >= ITERS
+        source = wide_out.at[exchange - ITERS] if wide else near_out.at[exchange]
+        target = wide_in.at[exchange - ITERS] if wide else near_in.at[exchange]
         copies = [
             send(
-                near_out.at[exchange, pair],
-                near_in.at[exchange, l],
+                source.at[pair],
+                target.at[l],
                 near_send.at[exchange, l],
                 near_recv.at[exchange, l],
                 device,
@@ -256,89 +261,146 @@
             for l, (pair, device) in enumerate(links)
         ]
         sent.extend(copies)
-        shaped = jnp.concatenate([field[:, :points], field[:, points:]], axis=0)
+        return copies
+
+    def bend(fields, bending):
+        halves = [f[:, i * points : (i + 1) * points] for f in fields for i in range(2)]
         curved = jnp.dot(
-            shaped, fourth, preferred_element_type=jnp.float32, precision=lax.Precision.HIGHEST
-        )
-        curved = jnp.concatenate([curved[:rows], curved[rows:]], axis=1)
-        image = field + bending * curved
-        if masks is None:
-            for copy in id_copies:
-                copy.wait_recv()
-            masks = targets_of(k)
-        image = image + masks[LINKS] * products[1]
+            jnp.concatenate(halves, axis=0),
+            fourth,
+            preferred_element_type=jnp.float32,
+            precision=lax.Precision.HIGHEST,
+        )
+        images = []
+        for j, field in enumerate(fields):
+            x_part = curved[2 * j * rows : (2 * j + 1) * rows]
+            y_part = curved[(2 * j + 1) * rows : (2 * j + 2) * rows]
+            images.append(field + bending * jnp.concatenate([x_part, y_part], axis=1))
+        return images
+
+    def receive(images, own, copies, exchange, masks):
+        wide = exchange >= ITERS
+        images = [image + masks[LINKS] * own[j : j + 1] for j, image in enumerate(images)]
         for l, copy in enumerate(copies):
             copy.wait_recv()
-            image = image + masks[l] * near_in[exchange, l]
-        return image * (1.0 / GAMMA), masks
-
-    def everywhere(values, which):
-        for t, (stage, inbox) in enumerate(zip(stages, (sum_in_0, sum_in_1, sum_in_2))):
-            if not stage:
-                continue
-            sum_out[which, t] = values
-            first = sum(len(s) for s in stages[:t])
-            copies = [
-                send(
-                    sum_out.at[which, t],
-                    inbox.at[which, i],
-                    sum_send.at[which, first + i],
-                    sum_recv.at[which, first + i],
-                    device,
-                )
-                for i, device in enumerate(stage)
+            arrived = wide_in[exchange - ITERS, l] if wide else near_in[exchange, l]
+            images = [
+                image + masks[l] * arrived[j : j + 1] for j, image in enumerate(images)
             ]
-            sent.extend(copies)
-            for i, copy in enumerate(copies):
-                copy.wait_recv()
-                values = values + inbox[which, i]
+        return [image * (1.0 / GAMMA) for image in images]
+
+    def folded(product):
+        wide = total_of(product[:, i * 128 : (i + 1) * 128] for i in range(columns // 128))
+        return jnp.sum(wide, axis=0, keepdims=True)
+
+    gram_pairs = [(i, j) for i in range(ITERS + 1) for j in range(i, ITERS + 1)]
+
+    def gram_sums(basis):
+        for n, (i, j) in enumerate(gram_pairs):
+            gram_buf[n : n + 1, :] = folded(basis[i] * basis[j])
+        sums = dot_nt(jnp.ones((8, 128), jnp.float32), gram_buf[...], lax.Precision.HIGHEST)
+        return sums[0:1]
+
+    order = [2, 0, 1]
+    inboxes = (sum_in_0, sum_in_1, sum_in_2)
+
+    def stage_start(values, which, t):
+        stage, inbox = stages[t], inboxes[t]
+        first = sum(len(s) for s in stages[:t])
+        sum_out[which, t] = values
+        copies = [
+            send(
+                sum_out.at[which, t],
+                inbox.at[which, i],
+                sum_send.at[which, first + i],
+                sum_recv.at[which, first + i],
+                device,
+            )
+            for i, device in enumerate(stage)
+        ]
+        sent.extend(copies)
+        return copies
+
+    def stage_end(values, copies, which, t):
+        for i, copy in enumerate(copies):
+            copy.wait_recv()
+            values = values + inboxes[t][which, i]
+        return values
+
+    def weights_of(values):
         diagonal = lax.broadcasted_iota(jnp.int32, (128, 128), 0) == lax.broadcasted_iota(
             jnp.int32, (128, 128), 1
         )
-        spread = jnp.dot(
+        scalar_buf[...] = jnp.dot(
             jnp.where(diagonal, values, 0.0),
             jnp.ones((128, 128), jnp.float32),
             preferred_element_type=jnp.float32,
             precision=lax.Precision.HIGHEST,
         )
-        scalar_buf[...] = spread
-
-    def folded(product):
-        wide = sum(product[:, i * 128 : (i + 1) * 128] for i in range(columns // 128))
-        return jnp.sum(wide, axis=0, keepdims=True)
+        weights = krylov_weights(
+            {pair: scalar_buf[n : n + 1, :] for n, pair in enumerate(gram_pairs)}
+        )
+        return [jnp.broadcast_to(weight[:, 0:1], (rows, columns)) for weight in weights]
+
+    def cross(field, j):
+        row_out[j] = jnp.sum(jnp.where(row_wide == slot, field, 0.0), axis=0, keepdims=True)
+        copy = send(row_out.at[j], row_in.at[j], row_send.at[j], row_recv.at[j], links[3][1])
+        sent.append(copy)
+        return copy
 
     gram_buf[...] = jnp.zeros_like(gram_buf)
-
-    def solve(start, bending, k, masks):
-        basis = [start]
-        for j in range(ITERS):
-            image, masks = apply(basis[j], bending, k, k * ITERS + j, masks)
-            basis.append(image)
-        pairs = [(i, j) for i in range(ITERS + 1) for j in range(i, ITERS + 1)]
-        for n, (i, j) in enumerate(pairs):
-            gram_buf[n : n + 1, :] = folded(basis[i] * basis[j])
-        sums = dot_nt(jnp.ones((8, 128), jnp.float32), gram_buf[...], lax.Precision.HIGHEST)
-        everywhere(sums[0:1], k)
-        weights = krylov_weights(
-            {pair: scalar_buf[n : n + 1, :] for n, pair in enumerate(pairs)}
-        )
-        return total_of(
-            jnp.broadcast_to(weights[a][:, 0:1], (rows, columns)) * basis[a] for a in range(ITERS)
-        )
-
-    for load in loads:
-        load.wait()
-    step_one = solve(pos_ref[...], stiff, 0, None)
-    row_out[0] = jnp.sum(jnp.where(row_wide == slot, step_one, 0.0), axis=0, keepdims=True)
-    crossing = send(row_out.at[0], row_in.at[0], row_send.at[0], row_recv.at[0], links[3][1])
-    sent.append(crossing)
-    masks = targets_of(1)
+    start = pos_ref[...]
+    loads[0].wait()
+    own = pick([start], 0, 0)
+    images = bend([start], stiff)
+
+    pl.semaphore_wait(barrier, len(greeted))
+    copies = launch(0)
+    id_copies = [
+        send(id_out, id_in.at[l], id_send.at[l], id_recv.at[l], device)
+        for l, (_, device) in enumerate(links)
+    ]
+    sent += id_copies
+    crossings = [cross(start, 0)]
+    loads[1].wait()
+    for copy in id_copies:
+        copy.wait_recv()
+    masks = targets_of(0)
+    later_masks = targets_of(1)
     new_stiff = jnp.sum(jnp.where(lane == 6, id_in[3], 0.0), axis=1, keepdims=True)
     moved_stiff = jnp.where(row_of == slot, new_stiff, stiff)
-    crossing.wait_recv()
-    crossed = jnp.where(row_wide == slot, row_in[0], step_one)
-    after_ref[...] = crossed
-    final_ref[...] = solve(crossed, moved_stiff, 1, masks)
+
+    basis = [start] + receive(images, own, copies, 0, masks)
+    for j in range(1, ITERS):
+        own = pick([basis[j]], 0, j)
+        copies = launch(j)
+        crossings.append(cross(basis[j], j))
+        images = bend([basis[j]], stiff)
+        basis += receive(images, own, copies, j, masks)
+
+    level = []
+    for j in range(ITERS):
+        crossings[j].wait_recv()
+        level.append(jnp.where(row_wide == slot, row_in[j], basis[j]))
+    levels = [level]
+    flying = None
+    for j in range(ITERS):
+        exchange = ITERS + j
+        own = pick(levels[j], 1, exchange)
+        copies = launch(exchange)
+        values = gram_sums(basis) if j == 0 else stage_end(values, flying, 0, order[j - 1])
+        flying = stage_start(values, 0, order[j])
+        images = bend(levels[j], moved_stiff)
+        levels.append(receive(images, own, copies, exchange, later_masks))
+    values = stage_end(values, flying, 0, order[ITERS - 1])
+    weights = weights_of(values)
+    second = [total_of(w * part for w, part in zip(weights, parts)) for parts in levels]
+    after_ref[...] = second[0]
+    values = gram_sums(second)
+    for t in order:
+        values = stage_end(values, stage_start(values, 1, t), 1, t)
+    weights = weights_of(values)
+    final_ref[...] = total_of(w * part for w, part in zip(weights, second))
     for copy in sent:
         copy.wait_send()
 
@@ -360,10 +422,12 @@
             pltpu.VMEM(blocks.shape, blocks.dtype),
             pltpu.VMEM((1, 128), f32),
             pltpu.VMEM((LINKS, 1, 128), f32),
-            pltpu.VMEM((2 * ITERS, PAIRS_IN, 1, columns), f32),
-            pltpu.VMEM((2 * ITERS, LINKS, 1, columns), f32),
-            pltpu.VMEM((1, 1, columns), f32),
-            pltpu.VMEM((1, 1, columns), f32),
+            pltpu.VMEM((ITERS, PAIRS_IN, 1, columns), f32),
+            pltpu.VMEM((ITERS, LINKS, 1, columns), f32),
+            pltpu.VMEM((ITERS, PAIRS_IN, 4, columns), f32),
+            pltpu.VMEM((ITERS, LINKS, 4, columns), f32),
+            pltpu.VMEM((ITERS, 1, columns), f32),
+            pltpu.VMEM((ITERS, 1, columns), f32),
             pltpu.VMEM((128, 128), f32),
             pltpu.VMEM((128, 128), f32),
             pltpu.VMEM((2, 3, 1, 128), f32),
@@ -375,8 +439,8 @@
             dma((LINKS,)),
             dma((2 * ITERS, LINKS)),
             dma((2 * ITERS, LINKS)),
-            dma((1,)),
-            dma((1,)),
+            dma((ITERS,)),
+            dma((ITERS,)),
             dma((2, sum(peers))),
             dma((2, sum(peers))),
         ],

time: 80.5 us -> 68.9 us (0.86)
  Pallas kernels: 76.2 us -> 64.6 us
    pallas_call x1, Pallas kernels: 76.2 us -> 64.6 us  [local(): pl.pallas_call(functools.partial(kernel, sizes), out_shape=(jax.ShapeDtyp...]
where the time goes in v2:
time: 68.9 us; the launch traced here: 68.7 us
  Pallas kernels  64.6 us (94%)
  local copies, waits for them, and re-layouts  2.75 us (4%)
  between operations  1.29 us (2%)
    pallas_call x1, Pallas kernels, local(): pl.pallas_call(functools.partial(kernel, sizes), out_shape=(jax.ShapeDtyp...  64.6 us
    unnamed x2, local copies, waits for them, and re-layouts  2.75 us

profile of v2, /device:TPU:1, one launch (start us, length us, event | category | flops | bytes accessed | tf_op | source)
XLA Modules:
  0.0 68.7 jit_solution(7224626114477918624)
XLA Ops:
  1.3 64.6 %shard_map.86 = (f32[16,512]{1,0:T(8,128)}, f32[16,512]{1,0:T(8,128)}) custom-call(s32[2,3]{1,0:T(2,128)} %src_ref.1, s32[2,3]{1,0:T(2,128)} %tgt_ref.1, s32[1,1]{1,0:T(1,128)S(6)} %copy.11.slot_ref, f32[16,512]{1,0:T(8,128)} %pos_ref.1, f32[1,16]{1,0:T(1,128)} %bitcast.1, f32[256,256]{1,0:T(8,128)} %constant.2.clone.fourth_ref, ...), custom_call_target="tpu_custom_call" | custom-call | tf_op jit(solution)/shard_map/pallas_call | solution.py:416
  65.9 1.4 %copy.12 = f32[16,512]{1,0:T(8,128)} copy(f32[16,512]{1,0:T(8,128)} %get-tuple-element.4) | data formatting | bytes 65536
  67.3 1.4 %copy.13 = f32[16,512]{1,0:T(8,128)} copy(f32[16,512]{1,0:T(8,128)} %get-tuple-element.5) | data formatting | bytes 65536

commit v3 on v2

--- a/solution.py
+++ b/solution.py
@@ -98,15 +98,21 @@
 
 def kernel(
     sizes,
+    src_any,
+    tgt_any,
+    slot_any,
+    pos_any,
+    stiff_any,
+    fourth_any,
+    blocks_ref,
+    after_ref,
+    final_ref,
     src_ref,
     tgt_ref,
     slot_ref,
     pos_ref,
     stiff_ref,
     fourth_ref,
-    blocks_ref,
-    after_ref,
-    final_ref,
     block_buf,
     id_out,
     id_in,
@@ -122,7 +128,9 @@
     sum_in_0,
     sum_in_1,
     sum_in_2,
+    load_sem,
     block_sem,
+    ready_sem,
     id_send,
     id_recv,
     near_send,
@@ -172,16 +180,50 @@
         [(y, lax.rem(z + i, nz), x, c, r) for i in range(1, nz)],
     ]
 
+    def around(distance):
+        steps = sorted({distance % nz, -distance % nz} - {0})
+        return [(y, lax.rem(z + step, nz), x, c, r) for step in steps]
+
+    barrier = pltpu.get_barrier_semaphore()
+    greeted = [device for _, device in links] + stages[0] + stages[1] + around(1)
+    for device in greeted:
+        pl.semaphore_signal(barrier, inc=1, device_id=device, device_id_type=MESH)
+
+    small = [
+        pltpu.make_async_copy(source, target, load_sem.at[n])
+        for n, (source, target) in enumerate(
+            (
+                (src_any, src_ref),
+                (tgt_any, tgt_ref),
+                (slot_any, slot_ref),
+                (stiff_any, stiff_ref),
+                (pos_any, pos_ref),
+                (fourth_any, fourth_ref),
+            )
+        )
+    ]
     loads = [
         pltpu.make_async_copy(blocks_ref.at[k], block_buf.at[k], block_sem.at[k]) for k in range(2)
     ]
-    for load in loads:
+    for load in small + loads:
         load.start()
 
-    barrier = pltpu.get_barrier_semaphore()
-    greeted = [device for _, device in links] + [device for stage in stages for device in stage]
-    for device in greeted:
-        pl.semaphore_signal(barrier, inc=1, device_id=device, device_id_type=MESH)
+    reach = [1]
+    while 2 * reach[-1] < nz:
+        reach.append(2 * reach[-1])
+    reach = reach[:-1] if len(reach) > 1 else []
+
+    def tell(n):
+        for device in around(reach[n]):
+            pl.semaphore_signal(
+                ready_sem.at[n], inc=1, device_id=device, device_id_type=MESH
+            )
+
+    def hear(n):
+        pl.semaphore_wait(ready_sem.at[n], len(around(reach[n])))
+
+    for load in small:
+        load.wait()
 
     lane = lax.broadcasted_iota(jnp.int32, (1, 128), 1)
     row_of = lax.broadcasted_iota(jnp.int32, (rows, 1), 0)
@@ -191,13 +233,26 @@
     )
     stiff_row = stiff_ref[...]
     stiff = jnp.sum(jnp.where(eye, stiff_row, 0.0), axis=1, keepdims=True)
-    slot = slot_ref[0, 0]
+    slot = slot_ref[...]
     leaving_stiff = jnp.sum(jnp.where(row_of == slot, stiff, 0.0), axis=0, keepdims=True)
 
+    pair_at = [lax.broadcasted_iota(jnp.int32, (2, PAIRS_IN), axis) for axis in range(2)]
+
+    def entry(ref, k, p):
+        chosen = (pair_at[0] == k) & (pair_at[1] == p)
+        row = jnp.sum(jnp.where(chosen, ref[...].astype(jnp.float32), 0.0), axis=1, keepdims=True)
+        return jnp.sum(row, axis=0, keepdims=True)
+
+    targets = {(k, p): entry(tgt_ref, k, p) for k in range(2) for p in range(PAIRS_IN)}
+    sources = {
+        (k, p): entry(src_ref, k, p).astype(jnp.int32) - own_base
+        for k in range(2)
+        for p in range(PAIRS_IN)
+    }
     ids = jnp.where(lane == 6, leaving_stiff, 0.0)
     for k in range(2):
         for p in range(PAIRS_IN):
-            ids = jnp.where(lane == k * PAIRS_IN + p, tgt_ref[k, p].astype(jnp.float32), ids)
+            ids = jnp.where(lane == k * PAIRS_IN + p, targets[k, p], ids)
     id_out[...] = ids
 
     def send(source, target, send_sem, recv_sem, device):
@@ -220,7 +275,7 @@
                 jnp.where(lane == k * PAIRS_IN + pair, id_in[l], 0.0), axis=1, keepdims=True
             )
             masks.append(row_of == target.astype(jnp.int32) - own_base)
-        masks.append(row_of == tgt_ref[k, 1] - own_base)
+        masks.append(row_of == targets[k, 1].astype(jnp.int32) - own_base)
         return [mask.astype(jnp.float32) for mask in masks]
 
     fourth = fourth_ref[...]
@@ -230,7 +285,7 @@
         out = near_out.at[exchange] if len(fields) == 1 else wide_out.at[exchange - ITERS]
         own = None
         for p in range(PAIRS_IN):
-            mask = row_wide == src_ref[k, p] - own_base
+            mask = row_wide == sources[k, p]
             stacked = jnp.zeros((8, columns), jnp.float32)
             for j, field in enumerate(fields):
                 picked = jnp.sum(jnp.where(mask, field, 0.0), axis=0, keepdims=True)
@@ -361,6 +416,8 @@
         for l, (_, device) in enumerate(links)
     ]
     sent += id_copies
+    if reach:
+        tell(0)
     crossings = [cross(start, 0)]
     loads[1].wait()
     for copy in id_copies:
@@ -375,9 +432,17 @@
         own = pick([basis[j]], 0, j)
         copies = launch(j)
         crossings.append(cross(basis[j], j))
+        if j - 1 < len(reach):
+            hear(j - 1)
+            if j < len(reach):
+                tell(j)
         images = bend([basis[j]], stiff)
         basis += receive(images, own, copies, j, masks)
 
+    for n in range(ITERS - 1, len(reach)):
+        hear(n)
+        if n + 1 < len(reach):
+            tell(n + 1)
     level = []
     for j in range(ITERS):
         crossings[j].wait_recv()
@@ -405,20 +470,30 @@
         copy.wait_send()
 
 
+def hand_over(after_in, final_in, after_ref, final_ref):
+    after_ref[...] = after_in[...]
+    final_ref[...] = final_in[...]
+
+
 def local(sizes, table, positions, stiffness, blocks, pair_src, pair_tgt, cross_slots):
     rows, columns = positions.shape
     ny, nz, nx, nc, nr = sizes
     peers = (nx * nc * nr - 1, ny - 1, nz - 1)
     vmem = pl.BlockSpec(memory_space=pltpu.VMEM)
-    smem = pl.BlockSpec(memory_space=pltpu.SMEM)
     f32 = jnp.float32
     dma = pltpu.SemaphoreType.DMA
-    return pl.pallas_call(
+    results = pl.pallas_call(
         functools.partial(kernel, sizes),
         out_shape=(jax.ShapeDtypeStruct((rows, columns), f32),) * 2,
-        in_specs=[smem, smem, smem, vmem, vmem, vmem, pl.BlockSpec(memory_space=pl.ANY)],
+        in_specs=[pl.BlockSpec(memory_space=pltpu.HBM)] * 7,
         out_specs=(vmem, vmem),
         scratch_shapes=[
+            pltpu.VMEM(pair_src.shape, jnp.int32),
+            pltpu.VMEM(pair_tgt.shape, jnp.int32),
+            pltpu.VMEM(cross_slots.shape, jnp.int32),
+            pltpu.VMEM((rows, columns), f32),
+            pltpu.VMEM((1, rows), f32),
+            pltpu.VMEM(table.shape, f32),
             pltpu.VMEM(blocks.shape, blocks.dtype),
             pltpu.VMEM((1, 128), f32),
             pltpu.VMEM((LINKS, 1, 128), f32),
@@ -434,7 +509,9 @@
             pltpu.VMEM((2, max(peers[0], 1), 1, 128), f32),
             pltpu.VMEM((2, max(peers[1], 1), 1, 128), f32),
             pltpu.VMEM((2, max(peers[2], 1), 1, 128), f32),
+            dma((6,)),
             dma((2,)),
+            pltpu.SemaphoreType.REGULAR((4,)),
             dma((LINKS,)),
             dma((LINKS,)),
             dma((2 * ITERS, LINKS)),
@@ -454,6 +531,12 @@
         jnp.asarray(table),
         blocks,
     )
+    return pl.pallas_call(
+        hand_over,
+        out_shape=(jax.ShapeDtypeStruct((rows, columns), f32),) * 2,
+        in_specs=[vmem, vmem],
+        out_specs=(vmem, vmem),
+    )(*results)
 
 
 def program(split):

time: 68.9 us -> 64.4 us (0.935)
  local copies, waits for them, and re-layouts: 2.75 us -> 0 us
  Pallas kernels: 64.6 us -> 62.9 us
    pallas_call x1, Pallas kernels: 64.6 us -> 61.5 us  [local(): pl.pallas_call(functools.partial(kernel, sizes), out_shape=(jax.ShapeDtyp...]
    unnamed x2 -> x0, local copies, waits for them, and re-layouts: 2.75 us -> none
    pallas_call x0 -> x1, Pallas kernels: none -> 1.4 us  [local(): pl.pallas_call(hand_over, out_shape=(jax.ShapeDtypeStruct((rows, columns)...]
where the time goes in v3:
time: 64.4 us; the launch traced here: 64.2 us
  Pallas kernels  62.9 us (98%)
  between operations  1.29 us (2%)
    pallas_call x1, Pallas kernels, local(): pl.pallas_call(functools.partial(kernel, sizes), out_shape=(jax.ShapeDtyp...  61.5 us
    pallas_call x1, Pallas kernels, local(): pl.pallas_call(hand_over, out_shape=(jax.ShapeDtypeStruct((rows, columns)...  1.4 us

profile of v3, /device:TPU:1, one launch (start us, length us, event | category | flops | bytes accessed | tf_op | source)
XLA Modules:
  0.0 64.2 jit_solution(4533786461127556317)
XLA Ops:
  1.3 61.5 %shard_map.86 = (f32[16,512]{1,0:T(8,128)}, f32[16,512]{1,0:T(8,128)}) custom-call(s32[2,3]{1,0:T(2,128)} %src_any.1, s32[2,3]{1,0:T(2,128)} %tgt_any.1, s32[1,1]{1,0:T(1,128)S(6)} %copy.9.slot_any, f32[16,512]{1,0:T(8,128)} %pos_any.1, f32[1,16]{1,0:T(1,128)} %bitcast.1, f32[256,256]{1,0:T(8,128)} %constant.2.clone.fourth_any, ...), custom_call_target="tpu_custom_call" | custom-call | tf_op jit(solution)/shard_map/pallas_call | solution.py:485
  62.8 1.4 %shard_map.87 = (f32[16,512]{1,0:T(8,128)}, f32[16,512]{1,0:T(8,128)}) custom-call(f32[16,512]{1,0:T(8,128)} %get-tuple-element.4.after_in, f32[16,512]{1,0:T(8,128)} %get-tuple-element.5.final_in), custom_call_target="tpu_custom_call" | custom-call | tf_op jit(solution)/shard_map/pallas_call | solution.py:534

commit v4 on v3

--- a/solution.py
+++ b/solution.py
@@ -127,7 +127,6 @@
     sum_out,
     sum_in_0,
     sum_in_1,
-    sum_in_2,
     load_sem,
     block_sem,
     ready_sem,
@@ -173,19 +172,24 @@
         for i in range(nx)
         for j in range(nc)
         for k in range(nr)
-    ][1:]
+    ]
     stages = [
-        [(y, z, a, b, d) for a, b, d in stage_0],
-        [(lax.rem(y + i, ny), z, x, c, r) for i in range(1, ny)],
+        [
+            (lax.rem(y + i, ny), z, a, b, d)
+            for i in range(ny)
+            for n, (a, b, d) in enumerate(stage_0)
+            if i or n
+        ],
         [(y, lax.rem(z + i, nz), x, c, r) for i in range(1, nz)],
     ]
+    columns_y = [(lax.rem(y + i, ny), z, x, c, r) for i in range(1, ny)]
 
     def around(distance):
         steps = sorted({distance % nz, -distance % nz} - {0})
         return [(y, lax.rem(z + step, nz), x, c, r) for step in steps]
 
     barrier = pltpu.get_barrier_semaphore()
-    greeted = [device for _, device in links] + stages[0] + stages[1] + around(1)
+    greeted = [device for _, device in links] + stages[0][: nx * nc * nr - 1] + columns_y + around(1)
     for device in greeted:
         pl.semaphore_signal(barrier, inc=1, device_id=device, device_id_type=MESH)
 
@@ -281,32 +285,27 @@
     fourth = fourth_ref[...]
     operand_row = lax.broadcasted_iota(jnp.int32, (8, columns), 0)
 
-    def pick(fields, k, exchange):
-        out = near_out.at[exchange] if len(fields) == 1 else wide_out.at[exchange - ITERS]
-        own = None
-        for p in range(PAIRS_IN):
-            mask = row_wide == sources[k, p]
-            stacked = jnp.zeros((8, columns), jnp.float32)
-            for j, field in enumerate(fields):
-                picked = jnp.sum(jnp.where(mask, field, 0.0), axis=0, keepdims=True)
-                stacked = jnp.where(lax.rem(operand_row, 4) == j, picked, stacked)
-            high = stacked.astype(jnp.bfloat16).astype(jnp.float32)
-            operand = jnp.where(operand_row < 4, high, stacked - high).astype(jnp.bfloat16)
-            product = dot_nt(operand, block_buf[k, p])
-            product = product[0:4] + product[4:8]
-            if len(fields) == 1:
-                product = product[0:1]
-            out[p] = product
-            if p == 1:
-                own = product
-        return own
-
-    def launch(exchange):
-        wide = exchange >= ITERS
-        source = wide_out.at[exchange - ITERS] if wide else near_out.at[exchange]
-        target = wide_in.at[exchange - ITERS] if wide else near_in.at[exchange]
-        copies = [
-            send(
+    def product_of(fields, k, p):
+        mask = row_wide == sources[k, p]
+        stacked = jnp.zeros((8, columns), jnp.float32)
+        for j, field in enumerate(fields):
+            picked = jnp.sum(jnp.where(mask, field, 0.0), axis=0, keepdims=True)
+            stacked = jnp.where(lax.rem(operand_row, 4) == j, picked, stacked)
+        high = stacked.astype(jnp.bfloat16).astype(jnp.float32)
+        operand = jnp.where(operand_row < 4, high, stacked - high).astype(jnp.bfloat16)
+        product = dot_nt(operand, block_buf[k, p])
+        product = product[0:4] + product[4:8]
+        return product[0:1] if len(fields) == 1 else product
+
+    def ends_of(exchange):
+        if exchange >= ITERS:
+            return wide_out.at[exchange - ITERS], wide_in.at[exchange - ITERS]
+        return near_out.at[exchange], near_in.at[exchange]
+
+    def launch(exchange, p):
+        source, target = ends_of(exchange)
+        copies = {
+            l: send(
                 source.at[pair],
                 target.at[l],
                 near_send.at[exchange, l],
@@ -314,9 +313,18 @@
                 device,
             )
             for l, (pair, device) in enumerate(links)
-        ]
-        sent.extend(copies)
+            if pair == p
+        }
+        sent.extend(copies.values())
         return copies
+
+    def dispatch(fields, k, exchange):
+        copies = {}
+        for p in (0, 2, 1):
+            own = product_of(fields, k, p)
+            ends_of(exchange)[0][p] = own
+            copies.update(launch(exchange, p))
+        return own, copies
 
     def bend(fields, bending):
         halves = [f[:, i * points : (i + 1) * points] for f in fields for i in range(2)]
@@ -336,8 +344,8 @@
     def receive(images, own, copies, exchange, masks):
         wide = exchange >= ITERS
         images = [image + masks[LINKS] * own[j : j + 1] for j, image in enumerate(images)]
-        for l, copy in enumerate(copies):
-            copy.wait_recv()
+        for l in sorted(copies):
+            copies[l].wait_recv()
             arrived = wide_in[exchange - ITERS, l] if wide else near_in[exchange, l]
             images = [
                 image + masks[l] * arrived[j : j + 1] for j, image in enumerate(images)
@@ -356,8 +364,8 @@
         sums = dot_nt(jnp.ones((8, 128), jnp.float32), gram_buf[...], lax.Precision.HIGHEST)
         return sums[0:1]
 
-    order = [2, 0, 1]
-    inboxes = (sum_in_0, sum_in_1, sum_in_2)
+    order = [1, 0]
+    inboxes = (sum_in_0, sum_in_1)
 
     def stage_start(values, which, t):
         stage, inbox = stages[t], inboxes[t]
@@ -406,11 +414,13 @@
     gram_buf[...] = jnp.zeros_like(gram_buf)
     start = pos_ref[...]
     loads[0].wait()
-    own = pick([start], 0, 0)
+    for p in (0, 2, 1):
+        own = product_of([start], 0, p)
+        near_out[0, p] = own
     images = bend([start], stiff)
 
     pl.semaphore_wait(barrier, len(greeted))
-    copies = launch(0)
+    copies = {l: copy for p in (0, 2, 1) for l, copy in launch(0, p).items()}
     id_copies = [
         send(id_out, id_in.at[l], id_send.at[l], id_recv.at[l], device)
         for l, (_, device) in enumerate(links)
@@ -418,6 +428,8 @@
     sent += id_copies
     if reach:
         tell(0)
+    for device in columns_y:
+        pl.semaphore_signal(ready_sem.at[3], inc=1, device_id=device, device_id_type=MESH)
     crossings = [cross(start, 0)]
     loads[1].wait()
     for copy in id_copies:
@@ -429,8 +441,7 @@
 
     basis = [start] + receive(images, own, copies, 0, masks)
     for j in range(1, ITERS):
-        own = pick([basis[j]], 0, j)
-        copies = launch(j)
+        own, copies = dispatch([basis[j]], 0, j)
         crossings.append(cross(basis[j], j))
         if j - 1 < len(reach):
             hear(j - 1)
@@ -439,6 +450,8 @@
         images = bend([basis[j]], stiff)
         basis += receive(images, own, copies, j, masks)
 
+    if columns_y:
+        pl.semaphore_wait(ready_sem.at[3], len(columns_y))
     for n in range(ITERS - 1, len(reach)):
         hear(n)
         if n + 1 < len(reach):
@@ -451,22 +464,30 @@
     flying = None
     for j in range(ITERS):
         exchange = ITERS + j
-        own = pick(levels[j], 1, exchange)
-        copies = launch(exchange)
-        values = gram_sums(basis) if j == 0 else stage_end(values, flying, 0, order[j - 1])
-        flying = stage_start(values, 0, order[j])
+        own, copies = dispatch(levels[j], 1, exchange)
+        if j == 0:
+            values = gram_sums(basis)
+        elif j <= len(order):
+            values = stage_end(values, flying, 0, order[j - 1])
+        if j < len(order):
+            flying = stage_start(values, 0, order[j])
+        elif j == len(order):
+            weights = weights_of(values)
         images = bend(levels[j], moved_stiff)
         levels.append(receive(images, own, copies, exchange, later_masks))
-    values = stage_end(values, flying, 0, order[ITERS - 1])
-    weights = weights_of(values)
     second = [total_of(w * part for w, part in zip(weights, parts)) for parts in levels]
     after_ref[...] = second[0]
     values = gram_sums(second)
+    done = list(sent)
     for t in order:
-        values = stage_end(values, stage_start(values, 1, t), 1, t)
+        flying = stage_start(values, 1, t)
+        if t == order[0]:
+            for copy in done:
+                copy.wait_send()
+        values = stage_end(values, flying, 1, t)
     weights = weights_of(values)
     final_ref[...] = total_of(w * part for w, part in zip(weights, second))
-    for copy in sent:
+    for copy in sent[len(done) :]:
         copy.wait_send()
 
 
@@ -478,7 +499,7 @@
 def local(sizes, table, positions, stiffness, blocks, pair_src, pair_tgt, cross_slots):
     rows, columns = positions.shape
     ny, nz, nx, nc, nr = sizes
-    peers = (nx * nc * nr - 1, ny - 1, nz - 1)
+    peers = (ny * nx * nc * nr - 1, nz - 1)
     vmem = pl.BlockSpec(memory_space=pltpu.VMEM)
     f32 = jnp.float32
     dma = pltpu.SemaphoreType.DMA
@@ -505,10 +526,9 @@
             pltpu.VMEM((ITERS, 1, columns), f32),
             pltpu.VMEM((128, 128), f32),
             pltpu.VMEM((128, 128), f32),
-            pltpu.VMEM((2, 3, 1, 128), f32),
+            pltpu.VMEM((2, 2, 1, 128), f32),
             pltpu.VMEM((2, max(peers[0], 1), 1, 128), f32),
             pltpu.VMEM((2, max(peers[1], 1), 1, 128), f32),
-            pltpu.VMEM((2, max(peers[2], 1), 1, 128), f32),
             dma((6,)),
             dma((2,)),
             pltpu.SemaphoreType.REGULAR((4,)),

time: 64.4 us -> 61.7 us (0.958)
  Pallas kernels: 62.9 us -> 60.2 us
    pallas_call x1, Pallas kernels: 61.5 us -> 58.8 us  [local(): pl.pallas_call(functools.partial(kernel, sizes), out_shape=(jax.ShapeDtyp...]
where the time goes in v4:
time: 61.7 us; the launch traced here: 61.5 us
  Pallas kernels  60.2 us (98%)
  between operations  1.29 us (2%)
    pallas_call x1, Pallas kernels, local(): pl.pallas_call(functools.partial(kernel, sizes), out_shape=(jax.ShapeDtyp...  58.8 us
    pallas_call x1, Pallas kernels, local(): pl.pallas_call(hand_over, out_shape=(jax.ShapeDtypeStruct((rows, columns)...  1.4 us

profile of v4, /device:TPU:1, one launch (start us, length us, event | category | flops | bytes accessed | tf_op | source)
XLA Modules:
  0.0 61.5 jit_solution(4494032101484691358)
XLA Ops:
  1.3 58.8 %shard_map.86 = (f32[16,512]{1,0:T(8,128)}, f32[16,512]{1,0:T(8,128)}) custom-call(s32[2,3]{1,0:T(2,128)} %src_any.1, s32[2,3]{1,0:T(2,128)} %tgt_any.1, s32[1,1]{1,0:T(1,128)S(6)} %copy.9.slot_any, f32[16,512]{1,0:T(8,128)} %pos_any.1, f32[1,16]{1,0:T(1,128)} %bitcast.1, f32[256,256]{1,0:T(8,128)} %constant.2.clone.fourth_any, ...), custom_call_target="tpu_custom_call" | custom-call | tf_op jit(solution)/shard_map/pallas_call | solution.py:506
  60.1 1.4 %shard_map.87 = (f32[16,512]{1,0:T(8,128)}, f32[16,512]{1,0:T(8,128)}) custom-call(f32[16,512]{1,0:T(8,128)} %get-tuple-element.4.after_in, f32[16,512]{1,0:T(8,128)} %get-tuple-element.5.final_in), custom_call_target="tpu_custom_call" | custom-call | tf_op jit(solution)/shard_map/pallas_call | solution.py:554

commit v5 on v4

--- a/solution.py
+++ b/solution.py
@@ -167,20 +167,31 @@
         (2, place(after, other)),
     ]
 
-    stage_0 = [
-        (lax.rem(x + i, nx), lax.rem(c + j, nc), lax.rem(r + k, nr))
-        for i in range(nx)
-        for j in range(nc)
-        for k in range(nr)
-    ]
+    def ring(step, size):
+        return min(step, size - step)
+
+    plane = sorted(
+        (
+            (-ring(i, ny) - (a if a else 2 * k), i, a, b, k)
+            for i in range(ny)
+            for a in range(nx)
+            for b in range(nc)
+            for k in range(nr)
+            if i or a or b or k
+        ),
+    )
+    at_plane = lambda i, a, b, k: (
+        lax.rem(y + i, ny),
+        z,
+        lax.rem(x + a, nx),
+        lax.rem(c + b, nc),
+        lax.rem(r + k, nr),
+    )
+    beside = [at_plane(*step) for _, *step in plane if step[0] == 0]
+    far_z = sorted(range(1, nz), key=lambda step: -ring(step, nz))
     stages = [
-        [
-            (lax.rem(y + i, ny), z, a, b, d)
-            for i in range(ny)
-            for n, (a, b, d) in enumerate(stage_0)
-            if i or n
-        ],
-        [(y, lax.rem(z + i, nz), x, c, r) for i in range(1, nz)],
+        [at_plane(*step) for _, *step in plane],
+        [(y, lax.rem(z + step, nz), x, c, r) for step in far_z],
     ]
     columns_y = [(lax.rem(y + i, ny), z, x, c, r) for i in range(1, ny)]
 
@@ -189,7 +200,7 @@
         return [(y, lax.rem(z + step, nz), x, c, r) for step in steps]
 
     barrier = pltpu.get_barrier_semaphore()
-    greeted = [device for _, device in links] + stages[0][: nx * nc * nr - 1] + columns_y + around(1)
+    greeted = [device for _, device in links] + beside + columns_y + around(1)
     for device in greeted:
         pl.semaphore_signal(barrier, inc=1, device_id=device, device_id_type=MESH)
 
@@ -358,11 +369,15 @@
 
     gram_pairs = [(i, j) for i in range(ITERS + 1) for j in range(i, ITERS + 1)]
 
+    diagonal = lax.broadcasted_iota(jnp.int32, (16, 128), 0) == lax.broadcasted_iota(
+        jnp.int32, (16, 128), 1
+    )
+
     def gram_sums(basis):
         for n, (i, j) in enumerate(gram_pairs):
             gram_buf[n : n + 1, :] = folded(basis[i] * basis[j])
-        sums = dot_nt(jnp.ones((8, 128), jnp.float32), gram_buf[...], lax.Precision.HIGHEST)
-        return sums[0:1]
+        sums = jnp.sum(gram_buf[...], axis=1, keepdims=True)
+        return jnp.sum(jnp.where(diagonal, sums, 0.0), axis=0, keepdims=True)
 
     order = [1, 0]
     inboxes = (sum_in_0, sum_in_1)
@@ -391,15 +406,8 @@
         return values
 
     def weights_of(values):
-        diagonal = lax.broadcasted_iota(jnp.int32, (128, 128), 0) == lax.broadcasted_iota(
-            jnp.int32, (128, 128), 1
-        )
-        scalar_buf[...] = jnp.dot(
-            jnp.where(diagonal, values, 0.0),
-            jnp.ones((128, 128), jnp.float32),
-            preferred_element_type=jnp.float32,
-            precision=lax.Precision.HIGHEST,
-        )
+        spread = jnp.sum(jnp.where(diagonal, values, 0.0), axis=1, keepdims=True)
+        scalar_buf[...] = jnp.broadcast_to(spread, scalar_buf.shape)
         weights = krylov_weights(
             {pair: scalar_buf[n : n + 1, :] for n, pair in enumerate(gram_pairs)}
         )
@@ -524,8 +532,8 @@
             pltpu.VMEM((ITERS, LINKS, 4, columns), f32),
             pltpu.VMEM((ITERS, 1, columns), f32),
             pltpu.VMEM((ITERS, 1, columns), f32),
-            pltpu.VMEM((128, 128), f32),
-            pltpu.VMEM((128, 128), f32),
+            pltpu.VMEM((16, 128), f32),
+            pltpu.VMEM((16, 128), f32),
             pltpu.VMEM((2, 2, 1, 128), f32),
             pltpu.VMEM((2, max(peers[0], 1), 1, 128), f32),
             pltpu.VMEM((2, max(peers[1], 1), 1, 128), f32),

time: 61.7 us -> 60.7 us (0.984)
  Pallas kernels: 60.2 us -> 59.2 us
    pallas_call x1, Pallas kernels: 58.8 us -> 57.8 us  [local(): pl.pallas_call(functools.partial(kernel, sizes), out_shape=(jax.ShapeDtyp...]
where the time goes in v5:
time: 60.7 us; the launch traced here: 60.5 us
  Pallas kernels  59.2 us (98%)
  between operations  1.29 us (2%)
    pallas_call x1, Pallas kernels, local(): pl.pallas_call(functools.partial(kernel, sizes), out_shape=(jax.ShapeDtyp...  57.8 us
    pallas_call x1, Pallas kernels, local(): pl.pallas_call(hand_over, out_shape=(jax.ShapeDtypeStruct((rows, columns)...  1.4 us

profile of v5, /device:TPU:1, one launch (start us, length us, event | category | flops | bytes accessed | tf_op | source)
XLA Modules:
  0.0 60.5 jit_solution(8694322354660256576)
XLA Ops:
  1.3 57.8 %shard_map.86 = (f32[16,512]{1,0:T(8,128)}, f32[16,512]{1,0:T(8,128)}) custom-call(s32[2,3]{1,0:T(2,128)} %src_any.1, s32[2,3]{1,0:T(2,128)} %tgt_any.1, s32[1,1]{1,0:T(1,128)S(6)} %copy.9.slot_any, f32[16,512]{1,0:T(8,128)} %pos_any.1, f32[1,16]{1,0:T(1,128)} %bitcast.1, f32[256,256]{1,0:T(8,128)} %constant.2.clone.fourth_any, ...), custom_call_target="tpu_custom_call" | custom-call | tf_op jit(solution)/shard_map/pallas_call | solution.py:514
  59.1 1.4 %shard_map.87 = (f32[16,512]{1,0:T(8,128)}, f32[16,512]{1,0:T(8,128)}) custom-call(f32[16,512]{1,0:T(8,128)} %get-tuple-element.4.after_in, f32[16,512]{1,0:T(8,128)} %get-tuple-element.5.final_in), custom_call_target="tpu_custom_call" | custom-call | tf_op jit(solution)/shard_map/pallas_call | solution.py:562

commit v6 on v5

--- a/solution.py
+++ b/solution.py
@@ -499,11 +499,6 @@
         copy.wait_send()
 
 
-def hand_over(after_in, final_in, after_ref, final_ref):
-    after_ref[...] = after_in[...]
-    final_ref[...] = final_in[...]
-
-
 def local(sizes, table, positions, stiffness, blocks, pair_src, pair_tgt, cross_slots):
     rows, columns = positions.shape
     ny, nz, nx, nc, nr = sizes
@@ -511,9 +506,9 @@
     vmem = pl.BlockSpec(memory_space=pltpu.VMEM)
     f32 = jnp.float32
     dma = pltpu.SemaphoreType.DMA
-    results = pl.pallas_call(
+    after_crossing, final_positions = pl.pallas_call(
         functools.partial(kernel, sizes),
-        out_shape=(jax.ShapeDtypeStruct((rows, columns), f32),) * 2,
+        out_shape=(pltpu.VMEM((rows, columns), f32),) * 2,
         in_specs=[pl.BlockSpec(memory_space=pltpu.HBM)] * 7,
         out_specs=(vmem, vmem),
         scratch_shapes=[
@@ -559,12 +554,7 @@
         jnp.asarray(table),
         blocks,
     )
-    return pl.pallas_call(
-        hand_over,
-        out_shape=(jax.ShapeDtypeStruct((rows, columns), f32),) * 2,
-        in_specs=[vmem, vmem],
-        out_specs=(vmem, vmem),
-    )(*results)
+    return after_crossing, final_positions
 
 
 def program(split):

time: 60.7 us -> 59.8 us (0.985)
  Pallas kernels: 59.2 us -> 57.2 us
  local copies, waits for them, and re-layouts: 0 us -> 1.23 us
    pallas_call x2 -> x1, Pallas kernels: 59.2 us -> 57.2 us  [local(): pl.pallas_call(functools.partial(kernel, sizes), out_shape=(pltpu.VMEM((r...]
    unnamed x0 -> x2, local copies, waits for them, and re-layouts: none -> 1.23 us
where the time goes in v6:
time: 59.8 us; the launch traced here: 59.7 us
  Pallas kernels  57.2 us (96%)
  between operations  1.29 us (2%)
  local copies, waits for them, and re-layouts  1.23 us (2%)
    pallas_call x1, Pallas kernels, local(): pl.pallas_call(functools.partial(kernel, sizes), out_shape=(pltpu.VMEM((r...  57.2 us
    unnamed x2, local copies, waits for them, and re-layouts  1.23 us

profile of v6, /device:TPU:1, one launch (start us, length us, event | category | flops | bytes accessed | tf_op | source)
XLA Modules:
  0.0 59.7 jit_solution(957013394212702348)
XLA Ops:
  1.3 57.2 %shard_map.86 = (f32[16,512]{1,0:T(8,128)S(1)}, f32[16,512]{1,0:T(8,128)S(1)}) custom-call(s32[2,3]{1,0:T(2,128)} %src_any.1, s32[2,3]{1,0:T(2,128)} %tgt_any.1, s32[1,1]{1,0:T(1,128)S(6)} %copy.13.slot_any, f32[16,512]{1,0:T(8,128)} %pos_any.1, f32[1,16]{1,0:T(1,128)} %bitcast.1, f32[256,256]{1,0:T(8,128)} %constant.2.clone.fourth_any, ...), custom_call_target="tpu_custom_call" | custom-call | tf_op jit(solution)/shard_map/pallas_call | solution.py:509
  58.5 0.6 %copy.11 = f32[16,512]{1,0:T(8,128)} copy(f32[16,512]{1,0:T(8,128)S(1)} %get-tuple-element.2) | data formatting | bytes 65536
  59.1 0.6 %copy.12 = f32[16,512]{1,0:T(8,128)} copy(f32[16,512]{1,0:T(8,128)S(1)} %get-tuple-element.3) | data formatting | bytes 65536
